TPU v7x, 32 devices: a whole 2x2x4 slice. The times are simulated.
32 devices in a mesh: half: 2 (over x), grp: 4 (over z), tile: 4 (over y, core).
Axes of the slice: x: 2, y: 2, z: 4, core: 2. Of those that a mesh axis runs over, the one named last changes fastest.
Arguments:
- core_tensor: bfloat16 [256, 96, 160], P(('half', 'grp', 'tile')), may hold values from -0.109375 to 0.109375
- term_operators: bfloat16 [32, 8, 8, 8], P(('half', 'grp', 'tile')), may hold values from -2 to 2
- block_terms: int32 [32, 8], P(('half', 'grp', 'tile')), may hold values from 0 to 8, as said below
- orbitals: bfloat16 [1024, 256, 256], P(('half', 'grp'), 'tile'), may hold values from -6 to 6
- potential: float32 [2, 8, 1024, 256], P(None, None, ('half', 'grp'), 'tile'), may hold values from -2.5 to 2.5
- kinetic: bfloat16 [1024, 1024], replicated, may hold values from -0.1875 to 0.1875
Outputs:
- h_orbitals: bfloat16 [1024, 256, 256], P(('half', 'grp'), 'tile')
Inputs may be any that keep to these rules, and one draw needn't show every extreme that they name: `block_terms`: each row lists distinct terms in its first slots and 8 in all later slots; every row lists at least one term, and some row lists 8 terms.
All inputs are finite; a program needn't handle non-finite values.
Results may differ from a plain program's by a relative error of at most 0.0056.
Values may be sent and summed in bfloat16 or wider, within the bound.
No kernel may reach another device: no remote copies, remote signals or barrier semaphores. Data moves between devices by JAX's collectives and lax.ppermute only.
A program may use at most 128 MiB of HBM per device.

v0:
```python
import jax
import jax.numpy as jnp
from jax import lax
from jax.sharding import PartitionSpec as P

TERMS = 8


def slot_sums(core_tensor, term_operators, block_terms):
    rows_tile, width_b, width_a = core_tensor.shape
    flat_core = core_tensor.reshape(rows_tile, width_b * width_a)
    listed = block_terms[0]
    live_slots = jnp.sum((listed < TERMS).astype(jnp.int32))
    labels = jnp.arange(TERMS, dtype=jnp.int32)

    def add_slot(slot_index, running):
        sum_a, sum_b = running
        operator = term_operators[0, slot_index]
        mixed_core = jnp.einsum(
            "rs,rq->sq", operator, flat_core, preferred_element_type=jnp.float32
        )
        mixed_core = mixed_core.astype(jnp.bfloat16).reshape(rows_tile, width_b, width_a)
        gram_a = jnp.einsum(
            "rba,rbc->ac", core_tensor, mixed_core, preferred_element_type=jnp.float32
        )
        gram_b = jnp.einsum(
            "rba,rda->bd", core_tensor, mixed_core, preferred_element_type=jnp.float32
        )
        chosen = (labels == listed[slot_index]).astype(jnp.float32)
        return (sum_a + chosen[:, None, None] * gram_a, sum_b + chosen[:, None, None] * gram_b)

    start_sums = (
        jnp.zeros((TERMS, width_a, width_a), jnp.float32),
        jnp.zeros((TERMS, width_b, width_b), jnp.float32),
    )
    return lax.fori_loop(0, live_slots, add_slot, start_sums)


def point_action(points, weights, stack_a, stack_b):
    width_a = stack_a.shape[0]
    width_b = stack_b.shape[0]
    count_points = points.shape[0]
    prod_a = jnp.dot(points[:, :width_a], stack_a, preferred_element_type=jnp.float32).reshape(
        count_points, TERMS, width_a
    )
    prod_b = jnp.dot(points[:, width_a:], stack_b, preferred_element_type=jnp.float32).reshape(
        count_points, TERMS, width_b
    )
    act_a = jnp.sum(prod_a * weights[0].T[:, :, None], axis=1)
    act_b = jnp.sum(prod_b * weights[1].T[:, :, None], axis=1)
    return jnp.concatenate([act_a, act_b], axis=1)


def kinetic_columns(kinetic, orbitals):
    rows_x, rows_y, width_all = orbitals.shape
    halves = lax.axis_size("half")
    members = lax.axis_size("grp")
    groups = halves * members
    columns = rows_y * width_all // groups
    pieces = orbitals.reshape(rows_x, groups, columns)
    applied = jnp.einsum(
        "xz,zik->xik",
        kinetic,
        lax.all_to_all(pieces, ("half", "grp"), split_axis=1, concat_axis=0, tiled=True),
        preferred_element_type=jnp.float32,
    )
    applied = applied.astype(jnp.bfloat16)
    returned = lax.all_to_all(applied, ("half", "grp"), split_axis=0, concat_axis=1, tiled=True)
    return returned.reshape(rows_x, rows_y, width_all)


def body(core_tensor, term_operators, block_terms, orbitals, potential, kinetic):
    sum_a, sum_b = slot_sums(core_tensor, term_operators, block_terms)
    total_a, total_b = lax.psum((sum_a, sum_b), ("half", "grp", "tile"))
    mean_a = total_a.astype(jnp.bfloat16)
    mean_b = total_b.astype(jnp.bfloat16)
    kinetic_part = kinetic_columns(kinetic, orbitals)
    rows_x, rows_y, width_all = orbitals.shape
    width_a = mean_a.shape[1]
    width_b = mean_b.shape[1]
    stack_a = jnp.transpose(mean_a, (1, 0, 2)).reshape(width_a, TERMS * width_a)
    stack_b = jnp.transpose(mean_b, (1, 0, 2)).reshape(width_b, TERMS * width_b)
    points = orbitals.reshape(rows_x * rows_y, width_all)
    weights = potential.reshape(2, TERMS, rows_x * rows_y)
    action = point_action(points, weights, stack_a, stack_b).reshape(rows_x, rows_y, width_all)
    return (kinetic_part.astype(jnp.float32) + action).astype(jnp.bfloat16)


def solution(mesh):
    return jax.shard_map(
        body,
        mesh=mesh,
        in_specs=(
            P(("half", "grp", "tile"), None, None),
            P(("half", "grp", "tile"), None, None, None),
            P(("half", "grp", "tile"), None),
            P(("half", "grp"), "tile", None),
            P(None, None, ("half", "grp"), "tile"),
            P(),
        ),
        out_specs=P(("half", "grp"), "tile", None),
        check_vma=False,
    )
```

profile of v0, /device:TPU:0, one launch (start us, length us, event | category | flops | bytes accessed | tf_op | source)
XLA Modules:
  0.0 330.5 jit_solution(8414382545134291300)
XLA Ops:
  0.0 7.0 %copy.53 = bf16[128,64,256]{0,2,1:T(8,128)(2,1)} copy(bf16[128,64,256]{2,1,0:T(8,128)(2,1)} %param.11) | data formatting | bytes 8388608 | tf_op args[3]
  7.0 7.4 %all-to-all-start = ((bf16[128,8,2048]{0,2,1:T(8,128)(2,1)}), bf16[128,8,2048]{0,2,1:T(8,128)(2,1)}, u32[]{:S(2)}, u32[]{:S(2)}) async-start(bf16[128,8,2048]{0,2,1:T(8,128)(2,1)} %bitcast.84), calls=%async_computation | async-start | bytes 8388608 | tf_op jit(solution)/shard_map/all_to_all | solution.py:64
  14.4 0.2 copy.57
  14.6 1.2 reshape.54
  15.9 0.6 fusion.9
  16.5 1.2 broadcast_in_dim.4
  17.7 17.9 %while.13 = (s32[]{:T(128)}, f32[8,160,160]{2,1,0:T(8,128)}, f32[8,96,96]{2,1,0:T(8,128)S(1)}, s32[]{:T(128)}, s32[8]{0:T(128)S(1)}, /*index=5*/bf16[1,8,8,8]{3,...) while((s32[]{:T(128)}, f32[8,160,160]{2,1,0:T(8,128)}, ...), condition=%wide.region_2.0_spmd.clone, body=%wide.region_1.0_spmd.clone.sunk | while | flops 65560596 | bytes 4753667 | solution.py:36
  18.3 1.2 convolution_convert_fusion.2
  19.5 0.5 reshape.69
  20.0 1.0 convolution_bitcast_fusion.4
  21.0 1.0 copy.70
  22.0 0.6 dynamic_slice.15
  22.6 0.6 compare_convert_fusion.3
  23.3 2.6 multiply_add_fusion.4
  25.9 0.3 convolution_bitcast_fusion.5
  27.0 1.2 convolution_convert_fusion.2
  28.2 0.5 reshape.69
  28.7 1.0 convolution_bitcast_fusion.4
  29.7 1.0 copy.70
  30.7 0.6 dynamic_slice.15
  31.3 0.6 compare_convert_fusion.3
  31.9 2.6 multiply_add_fusion.4
  34.5 0.3 convolution_bitcast_fusion.5
  35.6 120.4 %all-reduce.2 = (bf16[8,96,96]{2,1,0:T(8,128)(2,1)}, bf16[8,160,160]{2,1,0:T(8,128)(2,1)}) all-reduce(f32[8,96,96]{2,1,0:T(8,128)S(1)} %get-tuple-element.55, f32[8,160,160]{2,1,0:T(8,128)} %get-tuple-element.54), channel_id=1, replica_groups=mesh['half'=2,'grp'=4,'tile'=4] {'half','grp','tile'}, use_global_device_ids=true, to_apply=%region_5.0 | all-reduce | flops 278528 | bytes 1671168 | tf_op jit(solution)/shard_map/psum | solution.py:74
  156.1 1.5 copy.58
  157.5 0.7 reshape.55
  158.2 1.8 fusion.10
  160.4 1.0 copy.60
  161.4 0.8 reshape.58
  162.2 1.1 copy.61
  163.4 0.9 squeeze.17
  164.3 6.4 %copy.54 = bf16[8,128,1,2048]{3,1,0,2:T(8,128)(2,1)} copy(bf16[8,128,1,2048]{1,3,0,2:T(8,128)(2,1)} %bitcast.2) | data formatting | bytes 8388608 | tf_op jit(solution)/shard_map/all_to_all | solution.py:64
  170.7 8.2 %convert_bitcast_fusion = bf16[1024,1,2048]{2,0,1:T(8,128)(2,1)} fusion(bf16[1024,1024]{1,0:T(8,128)(2,1)S(1)} %copy-done, bf16[1024,2048]{1,0:T(8,128)(2,1)} %bitcast.85), kind=kOutput, calls=%fused_computation.17 | convolution fusion | flops 4297064448 | bytes 10485760 | tf_op jit(solution)/shard_map/xz,zik->xik/dot_general | solution.py:61
  178.9 0.5 broadcast.13
  179.4 6.8 %reduce = bf16[1024,2048]{1,0:T(8,128)(2,1)} reduce(bf16[1024,1,2048]{2,0,1:T(8,128)(2,1)} %convert_bitcast_fusion, bf16[]{:T(256)} %broadcast.13), dimensions={1}, to_apply=%copy.55.reduce_sub_computation | reduce | bytes 8388610 | tf_op jit(solution)/shard_map/convert_element_type | solution.py:67
  186.2 7.8 %reshape.66 = bf16[8,2,131072]{2,1,0:T(2,128)(2,1)} reshape(bf16[1024,2048]{1,0:T(8,128)(2,1)} %reduce) | data formatting | bytes 8388608
  194.0 4.9 %all-to-all-start.1 = ((bf16[8,2,131072]{2,1,0:T(2,128)(2,1)}), bf16[8,2,131072]{2,1,0:T(2,128)(2,1)}, u32[]{:S(2)}, u32[]{:S(2)}) async-start(bf16[8,2,131072]{2,1,0:T(2,128)(2,1)} %reshape.66), calls=%async_computation.1 | async-start | bytes 8388608 | tf_op jit(solution)/shard_map/all_to_all | solution.py:68
  198.9 11.9 %fusion.7 = f32[768,8192]{1,0:T(8,128)} fusion(bf16[96,768]{1,0:T(8,128)(2,1)S(1)} %copy-done.4, bf16[8192,256]{1,0:T(8,128)(2,1)} %bitcast.82), kind=kOutput, calls=%fused_computation.18 | convolution fusion | flops 1207959552 | bytes 27410432 | tf_op jit(solution)/shard_map/dot_general | solution.py:46
  210.8 11.6 %multiply_reduce_fusion.1 = f32[8192,96]{0,1:T(8,128)} fusion(f32[8192,8,96]{0,2,1:T(8,128)} %bitcast.78, f32[8192,8]{0,1:T(8,128)S(1)} %bitcast.87), kind=kLoop, calls=%fused_computation.11 | loop fusion | flops 11796480 | bytes 28573696 | tf_op jit(solution)/shard_map/reduce_sum | solution.py:50
  222.4 18.4 %fusion.5 = f32[1280,8192]{1,0:T(8,128)} fusion(bf16[160,1280]{1,0:T(8,128)(2,1)S(1)} %reshape.55, bf16[8192,256]{1,0:T(8,128)(2,1)} %bitcast.83), kind=kOutput, calls=%fused_computation.15 | convolution fusion | flops 3355443200 | bytes 46546944 | tf_op jit(solution)/shard_map/dot_general | solution.py:43
  240.8 18.2 %multiply_reduce_fusion = f32[8192,160]{0,1:T(8,128)} fusion(f32[8192,8,160]{0,2,1:T(8,128)} %bitcast.77, f32[8192,8]{0,1:T(8,128)S(1)} %bitcast.86), kind=kLoop, calls=%fused_computation.10 | loop fusion | flops 19660800 | bytes 47448064 | tf_op jit(solution)/shard_map/reduce_sum | solution.py:49
  259.0 7.6 %pad_maximum_fusion = f32[8192,256]{0,1:T(8,128)} fusion(f32[8192,96]{0,1:T(8,128)} %multiply_reduce_fusion.1, f32[8192,160]{0,1:T(8,128)} %multiply_reduce_fusion), kind=kLoop, calls=%fused_computation.12 | loop fusion | flops 2097152 | bytes 16777216 | tf_op jit(solution)/shard_map/concatenate | solution.py:51
  266.6 9.0 %copy.62 = f32[8192,256]{1,0:T(8,128)} copy(f32[8192,256]{0,1:T(8,128)} %pad_maximum_fusion) | data formatting | bytes 16777216 | tf_op jit(solution)/shard_map/concatenate | solution.py:51
  275.6 15.8 %all-to-all-done.1 = bf16[8,2,131072]{2,1,0:T(2,128)(2,1)} async-done(((bf16[8,2,131072]{2,1,0:T(2,128)(2,1)}), bf16[8,2,131072]{2,1,0:T(2,128)(2,1)}, u32[]{:S(2)}, u32[]{:S(2)}) %all-to-all-start.1) | async-done | bytes 4194336 | tf_op jit(solution)/shard_map/all_to_all | solution.py:68
  291.4 8.9 %reshape.67 = bf16[1024,1,2048]{2,1,0:T(2,128)(2,1)} reshape(bf16[8,2,131072]{2,1,0:T(2,128)(2,1)} %all-to-all-done.1) | data formatting | bytes 8388608
  300.2 11.5 %copy.66 = f32[8,128,1,2048]{3,0,1,2:T(8,128)} copy(bf16[8,128,1,2048]{3,2,1,0:T(2,128)(2,1)} %bitcast.80) | data formatting | bytes 12582912 | tf_op jit(solution)/shard_map/convert_element_type | solution.py:86
  311.7 9.3 %reshape.61 = f32[128,64,256]{2,1,0:T(8,128)} reshape(f32[128,8,1,2048]{3,1,0,2:T(8,128)} %bitcast.81) | data formatting | bytes 16777216 | tf_op jit(solution)/shard_map/convert_element_type | solution.py:86
  321.0 9.5 %add_convert_fusion = bf16[128,64,256]{2,1,0:T(8,128)(2,1)} fusion(f32[128,64,256]{2,1,0:T(8,128)} %reshape.61, f32[128,64,256]{2,1,0:T(8,128)} %bitcast.79), kind=kLoop, calls=%fused_computation.14 | loop fusion | flops 4194304 | bytes 20971520 | tf_op jit(solution)/shard_map/convert_element_type | solution.py:86
  (20 shorter events, 0.8 us)
Async XLA Ops:
  0.0 170.7 %copy-start = (bf16[1024,1024]{1,0:T(8,128)(2,1)S(1)}, bf16[1024,1024]{1,0:T(8,128)(2,1)}, u32[]{:S(2)}) copy-start(bf16[1024,1024]{1,0:T(8,128)(2,1)} %param.13) | copy-start | bytes 6291460
  7.0 7.4 %copy-start.2 = (bf16[8,96,160]{1,2,0:T(8,128)(2,1)S(1)}, bf16[8,96,160]{1,2,0:T(8,128)(2,1)}, u32[]{:S(2)}) copy-start(bf16[8,96,160]{1,2,0:T(8,128)(2,1)} %param.8) | copy-start | bytes 737284
  7.0 8.9 %copy-start.5 = (s32[1,8]{1,0:T(1,128)S(1)}, s32[1,8]{1,0:T(1,128)}, u32[]{:S(2)}) copy-start(s32[1,8]{1,0:T(1,128)} %param.10) | copy-start | bytes 100
  7.0 157.3 %all-to-all-start = ((bf16[128,8,2048]{0,2,1:T(8,128)(2,1)}), bf16[128,8,2048]{0,2,1:T(8,128)(2,1)}, u32[]{:S(2)}, u32[]{:S(2)}) async-start(bf16[128,8,2048]{0,2,1:T(8,128)(2,1)} %bitcast.84), calls=%async_computation | async-start | bytes 8388608 | tf_op jit(solution)/shard_map/all_to_all | solution.py:64
  194.0 4.9 %copy-start.4 = (bf16[96,768]{1,0:T(8,128)(2,1)S(1)}, bf16[96,768]{1,0:T(8,128)(2,1)}, u32[]{:S(2)}) copy-start(bf16[96,768]{1,0:T(8,128)(2,1)} %reshape.58) | copy-start | bytes 442372
  194.0 97.4 %all-to-all-start.1 = ((bf16[8,2,131072]{2,1,0:T(2,128)(2,1)}), bf16[8,2,131072]{2,1,0:T(2,128)(2,1)}, u32[]{:S(2)}, u32[]{:S(2)}) async-start(bf16[8,2,131072]{2,1,0:T(2,128)(2,1)} %reshape.66), calls=%async_computation.1 | async-start | bytes 8388608 | tf_op jit(solution)/shard_map/all_to_all | solution.py:68
  198.9 11.9 %copy-start.3 = (f32[8,8192]{1,0:T(8,128)S(1)}, f32[8,8192]{1,0:T(8,128)}, u32[]{:S(2)}) copy-start(f32[8,8192]{1,0:T(8,128)} %squeeze.17) | copy-start | bytes 786436
  321.0 9.5 %copy-start.1 = (bf16[1024,1024]{1,0:T(8,128)(2,1)S(1)}, bf16[1024,1024]{1,0:T(8,128)(2,1)}, u32[]{:S(2)}) copy-start(bf16[1024,1024]{1,0:T(8,128)(2,1)} %param.13) | copy-start | bytes 6291460
where the time goes:
time: 333 us; the launch traced here: 330 us
  blocking collectives  120 us (36%)
  local copies, waits for them, and re-layouts  75.6 us (23%)
  other arithmetic  61 us (18%)
  matrix products  43.4 us (13%)
  waiting for transfers between devices  15.8 us (5%)
  starting transfers between devices  12.3 us (4%)
    psum x1, blocking collectives, body(): total_a, total_b = lax.psum((sum_a, sum_b), ('half', 'grp', 'tile'))  120 us
    unnamed x16, local copies, waits for them, and re-layouts  23.9 us
    convert_element_type x2, local copies, waits for them, and re-layouts, body(): return (kinetic_part.astype(jnp.float32) + action).astype(jnp.bfloat16)  20.7 us
    dot_general x1, matrix products, point_action(): jnp.dot(points[:, :width_a], stack_a, preferred_element_type=jnp.float32)  18.4 us
    reduce_sum x1, other arithmetic, point_action(): act_a = jnp.sum(prod_a * weights[0].T[:, :, None], axis=1)  18.2 us
    all_to_all x1, waiting for transfers between devices, kinetic_columns(): lax.all_to_all(applied, ('half', 'grp'), split_axis=0, concat_axis=1, til...  15.8 us
    dot_general x1, matrix products, point_action(): jnp.dot(points[:, width_a:], stack_b, preferred_element_type=jnp.float32)  11.9 us
    reduce_sum x1, other arithmetic, point_action(): act_b = jnp.sum(prod_b * weights[1].T[:, :, None], axis=1)  11.6 us
  transfers between devices with their start and end apart: 2, of which 1 were waited for; matrix products, arithmetic and copies ran while one was open for 32% of the time, Pallas kernels for 0%

commit v1 on v0

--- a/solution.py
+++ b/solution.py
@@ -65,7 +65,15 @@
         preferred_element_type=jnp.float32,
     )
     applied = applied.astype(jnp.bfloat16)
-    returned = lax.all_to_all(applied, ("half", "grp"), split_axis=0, concat_axis=1, tiled=True)
+    returned = jnp.concatenate(
+        lax.all_to_all(
+            jnp.stack(jnp.split(applied, lax.axis_size(("half", "grp")), axis=0)),
+            ("half", "grp"),
+            0,
+            0,
+        ),
+        axis=1,
+    )
     return returned.reshape(rows_x, rows_y, width_all)
 
 

time: 333 us -> 316 us (0.949)
  waiting for transfers between devices: 15.8 us -> 6.64 us
  local copies, waits for them, and re-layouts: 75.6 us -> 69.3 us
    unnamed x16 -> x21, local copies, waits for them, and re-layouts: 23.9 us -> 13 us
    reshape x0 -> x1, local copies, waits for them, and re-layouts: none -> 9.24 us  [body(): point_action(points, weights, stack_a, stack_b)]
    all_to_all x1, waiting for transfers between devices: 15.8 us -> 6.64 us  [kinetic_columns(): lax.all_to_all(jnp.stack(jnp.split(applied, lax.axis_size(('half', 'grp')...]
    convert_element_type x1 -> x0, other arithmetic: 6.79 us -> none  [kinetic_columns(): applied = applied.astype(jnp.bfloat16)]
    convert_element_type x1 -> x2, other arithmetic: 9.5 us -> 16.1 us  [body(): return (kinetic_part.astype(jnp.float32) + action).astype(jnp.bfloat16)]
    convert_element_type x2, local copies, waits for them, and re-layouts: 20.7 us -> 15.8 us  [body(): return (kinetic_part.astype(jnp.float32) + action).astype(jnp.bfloat16)]
  transfers between devices with their start and end apart: 2 -> 2, of which waited for: 1 -> 1; matrix products, arithmetic and copies ran while one was open for 32% -> 36% of each run, Pallas kernels for 0% -> 0%
where the time goes in v1:
time: 316 us; the launch traced here: 314 us
  blocking collectives  120 us (38%)
  local copies, waits for them, and re-layouts  69.3 us (22%)
  other arithmetic  60.8 us (19%)
  matrix products  42.2 us (13%)
  starting transfers between devices  12.3 us (4%)
  waiting for transfers between devices  6.64 us (2%)
    psum x1, blocking collectives, body(): total_a, total_b = lax.psum((sum_a, sum_b), ('half', 'grp', 'tile'))  120 us
    dot_general x1, matrix products, point_action(): jnp.dot(points[:, :width_a], stack_a, preferred_element_type=jnp.float32)  18.4 us
    reduce_sum x1, other arithmetic, point_action(): act_a = jnp.sum(prod_a * weights[0].T[:, :, None], axis=1)  18.2 us
    convert_element_type x2, other arithmetic, body(): return (kinetic_part.astype(jnp.float32) + action).astype(jnp.bfloat16)  16.1 us
    convert_element_type x2, local copies, waits for them, and re-layouts, body(): return (kinetic_part.astype(jnp.float32) + action).astype(jnp.bfloat16)  15.8 us
    unnamed x21, local copies, waits for them, and re-layouts  13 us
    dot_general x1, matrix products, point_action(): jnp.dot(points[:, width_a:], stack_b, preferred_element_type=jnp.float32)  11.9 us
    reduce_sum x1, other arithmetic, point_action(): act_b = jnp.sum(prod_b * weights[1].T[:, :, None], axis=1)  11.6 us
  transfers between devices with their start and end apart: 2, of which 1 were waited for; matrix products, arithmetic and copies ran while one was open for 36% of the time, Pallas kernels for 0%

profile of v1, /device:TPU:0, one launch (start us, length us, event | category | flops | bytes accessed | tf_op | source)
XLA Modules:
  0.0 313.7 jit_solution(13755656041056892793)
XLA Ops:
  0.0 7.0 %copy.41 = bf16[128,64,256]{0,2,1:T(8,128)(2,1)} copy(bf16[128,64,256]{2,1,0:T(8,128)(2,1)} %param.11) | data formatting | bytes 8388608 | tf_op args[3]
  7.0 7.4 %all-to-all-start = ((bf16[128,8,2048]{0,2,1:T(8,128)(2,1)}), bf16[128,8,2048]{0,2,1:T(8,128)(2,1)}, u32[]{:S(2)}, u32[]{:S(2)}) async-start(bf16[128,8,2048]{0,2,1:T(8,128)(2,1)} %bitcast.107), calls=%async_computation | async-start | bytes 8388608 | tf_op jit(solution)/shard_map/all_to_all | solution.py:64
  14.6 1.2 reshape.67
  15.8 0.7 fusion.17
  16.5 1.2 broadcast_in_dim.4
  17.7 18.0 %while.13 = (s32[]{:T(128)}, f32[8,160,160]{2,1,0:T(8,128)}, f32[8,96,96]{2,1,0:T(8,128)S(1)}, s32[]{:T(128)}, s32[8]{0:T(128)S(1)}, /*index=5*/bf16[1,8,8,8]{3,...) while((s32[]{:T(128)}, f32[8,160,160]{2,1,0:T(8,128)}, ...), condition=%wide.region_2.0_spmd.clone, body=%wide.region_1.0_spmd.clone.sunk | while | flops 65560596 | bytes 4753667 | solution.py:36
  18.4 1.2 convolution_convert_fusion.3
  20.1 1.0 convolution_bitcast_fusion.4
  21.1 1.0 copy.56
  22.1 0.6 dynamic_slice.15
  22.7 0.6 compare_convert_fusion.3
  23.3 2.6 multiply_add_fusion.4
  27.0 1.2 convolution_convert_fusion.3
  28.8 1.0 convolution_bitcast_fusion.4
  29.7 1.0 copy.56
  30.8 0.6 dynamic_slice.15
  31.9 2.6 multiply_add_fusion.4
  35.7 120.3 %all-reduce.2 = (bf16[8,96,96]{2,1,0:T(8,128)(2,1)}, bf16[8,160,160]{2,1,0:T(8,128)(2,1)}) all-reduce(f32[8,96,96]{2,1,0:T(8,128)S(1)} %get-tuple-element.55, f32[8,160,160]{2,1,0:T(8,128)} %get-tuple-element.54), channel_id=1, replica_groups=mesh['half'=2,'grp'=4,'tile'=4] {'half','grp','tile'}, use_global_device_ids=true, to_apply=%region_5.0 | all-reduce | flops 278528 | bytes 1671168 | tf_op jit(solution)/shard_map/psum | solution.py:82
  156.0 1.5 copy.45
  157.5 0.7 reshape.68
  158.2 1.8 fusion.18
  160.3 1.0 copy.47
  161.3 0.8 reshape.71
  162.2 1.1 copy.48
  163.3 0.9 squeeze.17
  164.3 6.4 %copy.42 = bf16[8,128,1,2048]{3,1,0,2:T(8,128)(2,1)} copy(bf16[8,128,1,2048]{1,3,0,2:T(8,128)(2,1)} %bitcast.2) | data formatting | bytes 8388608 | tf_op jit(solution)/shard_map/all_to_all | solution.py:64
  170.7 6.9 %convolution_convert_fusion.1 = bf16[1024,2048]{1,0:T(8,128)(2,1)S(1)} fusion(bf16[1024,1024]{1,0:T(8,128)(2,1)S(1)} %copy-done, bf16[1024,2048]{1,0:T(8,128)(2,1)} %bitcast.108), kind=kOutput, calls=%fused_computation.17 | convolution fusion | flops 4297064448 | bytes 10485760 | tf_op jit(solution)/shard_map/xz,zik->xik/dot_general | solution.py:61
  177.6 0.8 fusion.16
  178.4 0.8 fusion.15
  179.2 0.8 fusion.14
  180.1 0.8 fusion.13
  180.9 0.8 fusion.12
  181.7 0.8 fusion.11
  182.6 0.8 fusion.10
  183.4 0.8 fusion.9
  184.2 4.9 %all-to-all-start.1 = ((bf16[8,128,1,2048]{3,1,2,0:T(8,128)(2,1)}), bf16[8,128,1,2048]{3,1,2,0:T(8,128)(2,1)}, u32[]{:S(2)}, u32[]{:S(2)}) async-start(bf16[8,128,1,2048]{3,1,2,0:T(8,128)(2,1)} %fusion.9), calls=%async_computation.1 | async-start | bytes 8388608 | tf_op jit(solution)/shard_map/all_to_all | solution.py:69
  189.1 11.9 %fusion.7 = f32[768,8192]{1,0:T(8,128)} fusion(bf16[96,768]{1,0:T(8,128)(2,1)S(1)} %copy-done.4, bf16[8192,256]{1,0:T(8,128)(2,1)} %bitcast.105), kind=kOutput, calls=%fused_computation.18 | convolution fusion | flops 1207959552 | bytes 27410432 | tf_op jit(solution)/shard_map/dot_general | solution.py:46
  201.0 11.6 %multiply_reduce_fusion.1 = f32[8192,96]{0,1:T(8,128)} fusion(f32[8192,8,96]{0,2,1:T(8,128)} %bitcast.102, f32[8192,8]{0,1:T(8,128)S(1)} %bitcast.110), kind=kLoop, calls=%fused_computation.11 | loop fusion | flops 11796480 | bytes 28573696 | tf_op jit(solution)/shard_map/reduce_sum | solution.py:50
  212.6 18.4 %fusion.5 = f32[1280,8192]{1,0:T(8,128)} fusion(bf16[160,1280]{1,0:T(8,128)(2,1)S(1)} %reshape.68, bf16[8192,256]{1,0:T(8,128)(2,1)} %bitcast.106), kind=kOutput, calls=%fused_computation.15 | convolution fusion | flops 3355443200 | bytes 46546944 | tf_op jit(solution)/shard_map/dot_general | solution.py:43
  231.1 18.2 %multiply_reduce_fusion = f32[8192,160]{0,1:T(8,128)} fusion(f32[8192,8,160]{0,2,1:T(8,128)} %bitcast.101, f32[8192,8]{0,1:T(8,128)S(1)} %bitcast.109), kind=kLoop, calls=%fused_computation.10 | loop fusion | flops 19660800 | bytes 47448064 | tf_op jit(solution)/shard_map/reduce_sum | solution.py:49
  249.3 7.6 %pad_maximum_fusion = f32[8192,256]{0,1:T(8,128)} fusion(f32[8192,96]{0,1:T(8,128)} %multiply_reduce_fusion.1, f32[8192,160]{0,1:T(8,128)} %multiply_reduce_fusion), kind=kLoop, calls=%fused_computation.12 | loop fusion | flops 2097152 | bytes 16777216 | tf_op jit(solution)/shard_map/concatenate | solution.py:51
  256.8 9.0 %copy.49 = f32[8192,256]{1,0:T(8,128)} copy(f32[8192,256]{0,1:T(8,128)} %pad_maximum_fusion) | data formatting | bytes 16777216 | tf_op jit(solution)/shard_map/concatenate | solution.py:51
  265.8 9.2 %copy.50 = f32[128,64,256]{0,2,1:T(8,128)} copy(f32[128,64,256]{2,1,0:T(8,128)} %bitcast.104) | data formatting | bytes 16777216 | tf_op jit(solution)/shard_map/reshape | solution.py:93
  275.1 6.6 %all-to-all-done.1 = bf16[8,128,1,2048]{3,1,2,0:T(8,128)(2,1)} async-done(((bf16[8,128,1,2048]{3,1,2,0:T(8,128)(2,1)}), bf16[8,128,1,2048]{3,1,2,0:T(8,128)(2,1)}, u32[]{:S(2)}, u32[]{:S(2)}) %all-to-all-start.1) | async-done | bytes 4194336 | tf_op jit(solution)/shard_map/all_to_all | solution.py:69
  281.7 6.5 %convert_bitcast_fusion = f32[128,8,1,2048]{3,0,2,1:T(8,128)} fusion(bf16[8,128,1,2048]{3,1,2,0:T(8,128)(2,1)} %all-to-all-done.1), kind=kLoop, calls=%fused_computation.13 | loop fusion | flops 2097152 | bytes 12582912 | tf_op jit(solution)/shard_map/convert_element_type | solution.py:94
  288.2 9.1 %copy.43 = f32[128,8,1,2048]{0,3,1,2:T(8,128)} copy(f32[128,8,1,2048]{3,0,2,1:T(8,128)} %convert_bitcast_fusion) | data formatting | bytes 16777216 | tf_op jit(solution)/shard_map/convert_element_type | solution.py:94
  297.3 9.6 %add_convert_fusion = bf16[128,64,256]{0,2,1:T(8,128)(2,1)} fusion(f32[128,64,256]{0,2,1:T(8,128)} %bitcast.103, f32[128,64,256]{0,2,1:T(8,128)} %copy.50), kind=kLoop, calls=%fused_computation.14 | loop fusion | flops 4194304 | bytes 20971520 | tf_op jit(solution)/shard_map/convert_element_type | solution.py:94
  307.0 6.7 %copy.51 = bf16[128,64,256]{2,1,0:T(8,128)(2,1)} copy(bf16[128,64,256]{0,2,1:T(8,128)(2,1)} %add_convert_fusion) | data formatting | bytes 8388608 | tf_op jit(solution)/shard_map/convert_element_type | solution.py:94
  (26 shorter events, 3.2 us)
Async XLA Ops:
  0.0 170.7 %copy-start = (bf16[1024,1024]{1,0:T(8,128)(2,1)S(1)}, bf16[1024,1024]{1,0:T(8,128)(2,1)}, u32[]{:S(2)}) copy-start(bf16[1024,1024]{1,0:T(8,128)(2,1)} %param.13) | copy-start | bytes 6291460
  7.0 7.4 %copy-start.2 = (bf16[8,96,160]{1,2,0:T(8,128)(2,1)S(1)}, bf16[8,96,160]{1,2,0:T(8,128)(2,1)}, u32[]{:S(2)}) copy-start(bf16[8,96,160]{1,2,0:T(8,128)(2,1)} %param.8) | copy-start | bytes 737284
  7.0 8.9 %copy-start.5 = (s32[1,8]{1,0:T(1,128)S(1)}, s32[1,8]{1,0:T(1,128)}, u32[]{:S(2)}) copy-start(s32[1,8]{1,0:T(1,128)} %param.10) | copy-start | bytes 100
  7.0 157.3 %all-to-all-start = ((bf16[128,8,2048]{0,2,1:T(8,128)(2,1)}), bf16[128,8,2048]{0,2,1:T(8,128)(2,1)}, u32[]{:S(2)}, u32[]{:S(2)}) async-start(bf16[128,8,2048]{0,2,1:T(8,128)(2,1)} %bitcast.107), calls=%async_computation | async-start | bytes 8388608 | tf_op jit(solution)/shard_map/all_to_all | solution.py:64
  184.2 4.9 %copy-start.4 = (bf16[96,768]{1,0:T(8,128)(2,1)S(1)}, bf16[96,768]{1,0:T(8,128)(2,1)}, u32[]{:S(2)}) copy-start(bf16[96,768]{1,0:T(8,128)(2,1)} %reshape.71) | copy-start | bytes 442372
  184.2 97.5 %all-to-all-start.1 = ((bf16[8,128,1,2048]{3,1,2,0:T(8,128)(2,1)}), bf16[8,128,1,2048]{3,1,2,0:T(8,128)(2,1)}, u32[]{:S(2)}, u32[]{:S(2)}) async-start(bf16[8,128,1,2048]{3,1,2,0:T(8,128)(2,1)} %fusion.9), calls=%async_computation.1 | async-start | bytes 8388608 | tf_op jit(solution)/shard_map/all_to_all | solution.py:69
  189.1 11.9 %copy-start.3 = (f32[8,8192]{1,0:T(8,128)S(1)}, f32[8,8192]{1,0:T(8,128)}, u32[]{:S(2)}) copy-start(f32[8,8192]{1,0:T(8,128)} %squeeze.17) | copy-start | bytes 786436
  297.3 16.3 %copy-start.1 = (bf16[1024,1024]{1,0:T(8,128)(2,1)S(1)}, bf16[1024,1024]{1,0:T(8,128)(2,1)}, u32[]{:S(2)}) copy-start(bf16[1024,1024]{1,0:T(8,128)(2,1)} %param.13) | copy-start | bytes 6291460
